TPU v7x, 32 devices: a whole 2x2x4 slice. The times are simulated.
32 devices in a mesh: fsdp: 2 (over x), context: 4 (over y, core), tensor: 4 (over z).
Axes of the slice: x: 2, y: 2, z: 4, core: 2. Of those that a mesh axis runs over, the one named last changes fastest.
Arguments:
- hidden_in: bfloat16 [2, 1024, 2048], P('fsdp', ('context', 'tensor')), may hold values from -6 to 6
- segment_ids: int32 [2, 1024], P('fsdp'), may hold values from 0 to 15, never falling along the last dimension, each value on 1 to 512 neighbouring positions
- pad_mask: int32 [2, 1024], P('fsdp'), may hold values from 0 to 1, as said below
- attn_gain: bfloat16 [2048], P(('fsdp', 'context')), may hold values from 0.5 to 1.5
- w_query: bfloat16 [2048, 2048], P(('fsdp', 'context'), 'tensor'), may hold values from -0.1875 to 0.1875
- w_key: bfloat16 [2048, 256], P(('fsdp', 'context'), 'tensor'), may hold values from -0.1875 to 0.1875
- w_value: bfloat16 [2048, 256], P(('fsdp', 'context'), 'tensor'), may hold values from -0.125 to 0.125
- w_out: bfloat16 [2048, 2048], P('tensor', ('fsdp', 'context')), may hold values from -0.5 to 0.5
- mlp_gain: bfloat16 [2048], P(('fsdp', 'context')), may hold values from 0.5 to 1.5
- w_gate: bfloat16 [2048, 5632], P(('fsdp', 'context'), 'tensor'), may hold values from -0.125 to 0.125
- w_up: bfloat16 [2048, 5632], P(('fsdp', 'context'), 'tensor'), may hold values from -0.125 to 0.125
- w_down: bfloat16 [5632, 2048], P('tensor', ('fsdp', 'context')), may hold values from -0.078125 to 0.078125
- cotangent: bfloat16 [2, 1024, 2048], P('fsdp', ('context', 'tensor')), may hold values from -6 to 6
Outputs:
- block_out: bfloat16 [2, 1024, 2048], P('fsdp', ('context', 'tensor'))
- grad_hidden: float32 [2, 1024, 2048], P('fsdp', ('context', 'tensor'))
- grad_attn_gain: float32 [2048], P(('fsdp', 'context'))
- grad_query: float32 [2048, 2048], P(('fsdp', 'context'), 'tensor')
- grad_key: float32 [2048, 256], P(('fsdp', 'context'), 'tensor')
- grad_value: float32 [2048, 256], P(('fsdp', 'context'), 'tensor')
- grad_out: float32 [2048, 2048], P('tensor', ('fsdp', 'context'))
- grad_mlp_gain: float32 [2048], P(('fsdp', 'context'))
- grad_gate: float32 [2048, 5632], P(('fsdp', 'context'), 'tensor')
- grad_up: float32 [2048, 5632], P(('fsdp', 'context'), 'tensor')
- grad_down: float32 [5632, 2048], P('tensor', ('fsdp', 'context'))
Inputs may be any that keep to these rules, and one draw needn't show every extreme that they name: `segment_ids`: ids never fall along a sequence; a document is a run of 1 to 512 consecutive tokens of one id. `pad_mask`: every sequence ends in one or more padding slots, and no other slot is padding.
All inputs are finite; a program needn't handle non-finite values.
Results may differ from a plain program's by a relative error of at most 0.013.
The roundings to bfloat16 on the way count: a program that leaves them out, or rounds other values in their place, can miss the bound.
Values may be sent and summed in bfloat16 or wider, within the bound.
A program may use at most 88 MiB of HBM per device.

v0:
```python
import math
import jax
import jax.numpy as jnp
from jax import lax
from jax.sharding import PartitionSpec as P

EPS = 1e-05
NEG = -1e30
BF = jnp.bfloat16
F32 = jnp.float32


def rope_tables(positions, head_size):
    half_size = head_size // 2
    frequency = jnp.exp(-(jnp.arange(half_size, dtype=F32) * (2.0 / head_size)) * math.log(10000.0))
    angles = positions.astype(F32)[..., None] * frequency
    return (jnp.cos(angles)[..., None, :], jnp.sin(angles)[..., None, :])


def rotate(vectors, cos_table, sin_table):
    half_size = vectors.shape[-1] // 2
    first_half = vectors[..., :half_size]
    second_half = vectors[..., half_size:]
    return jnp.concatenate(
        [
            first_half * cos_table - second_half * sin_table,
            second_half * cos_table + first_half * sin_table,
        ],
        axis=-1,
    )


def mm(a, b, ca=1, cb=0):
    return lax.dot_general(a, b, (((ca,), (cb,)), ((), ())), preferred_element_type=F32)


def rows_gather(x):
    return lax.all_gather(x, "tensor", axis=0, tiled=True)


def rows_sum(x):
    return lax.psum_scatter(x.astype(BF), "tensor", scatter_dimension=0, tiled=True).astype(F32)


FC = ("fsdp", "context")


def gather_w(w, axis=0):
    return lax.all_gather(w, FC, axis=axis, tiled=True)


def scatter_g(g, axis=0):
    return lax.psum_scatter(g.astype(BF), FC, scatter_dimension=axis, tiled=True).astype(F32)


def norm_back(grad_normed, vectors, inv_scale, gain_row):
    unit_rows = vectors * inv_scale
    weighted = grad_normed * gain_row
    grad_gain = jnp.sum(grad_normed * unit_rows, axis=0)
    grad_vectors = inv_scale * (
        weighted - unit_rows * jnp.mean(weighted * unit_rows, axis=-1, keepdims=True)
    )
    return (grad_vectors, grad_gain)


def one_sequence(
    hidden_in,
    segment_ids,
    pad_mask,
    attn_gain,
    w_query,
    w_key,
    w_value,
    w_out,
    mlp_gain,
    w_gate,
    w_up,
    w_down,
    cotangent,
):
    row_count, model_width = hidden_in.shape
    context_count = lax.axis_size("context")
    tensor_count = lax.axis_size("tensor")
    context_index = lax.axis_index("context")
    tensor_index = lax.axis_index("tensor")
    length = segment_ids.shape[0]
    span = length // context_count
    hd = w_key.shape[1]
    start = context_index * span
    seg_span = lax.dynamic_slice_in_dim(segment_ids, start, span, 0)
    columns = jnp.arange(length, dtype=jnp.int32)
    row_at = start + jnp.arange(span, dtype=jnp.int32)
    first = jnp.sum((segment_ids[None, :] < seg_span[:, None]).astype(jnp.int32), axis=1)
    cos_t, sin_t = rope_tables(row_at - first, hd)
    row_start = start + tensor_index * row_count
    keep = lax.dynamic_slice_in_dim(pad_mask, row_start, row_count, 0).astype(F32)[:, None]
    allowed = (
        (seg_span[:, None] == segment_ids[None, :])
        & (columns[None, :] <= row_at[:, None])
        & ((pad_mask[None, :] == 1) | (columns[None, :] == row_at[:, None]))
    )
    gain_one = gather_w(attn_gain).astype(F32)
    gain_two = gather_w(mlp_gain).astype(F32)
    qkv_all = gather_w(jnp.concatenate([w_query, w_key, w_value], axis=1))
    out_all = gather_w(w_out, 1)
    gate_all = gather_w(w_gate)
    up_all = gather_w(w_up)
    down_all = gather_w(w_down, 1)
    qw = w_query.shape[1]
    hidden = hidden_in.astype(F32)
    scale_one = lax.rsqrt(jnp.mean(hidden * hidden, axis=-1, keepdims=True) + EPS)
    n1 = rows_gather((hidden * scale_one * gain_one).astype(BF))
    g_out = cotangent.astype(F32) * keep
    g_all = rows_gather(g_out.astype(BF))
    pre = mm(n1, qkv_all)
    q = rotate(pre[:, :qw].reshape(span, -1, hd), cos_t, sin_t).astype(BF)
    k = rotate(pre[:, None, qw : qw + hd], cos_t, sin_t).astype(BF)[:, 0]
    v = pre[:, qw + hd :].astype(BF)
    kv = lax.all_gather(jnp.concatenate([k, v], axis=1), "context", axis=0, tiled=True)
    k, v = (kv[:, :hd], kv[:, hd:])
    scale = hd ** (-0.5)
    scores = jnp.einsum("qhd,td->hqt", q, k, preferred_element_type=F32) * scale
    scores = jnp.where(allowed[None], scores, NEG)
    top = jnp.max(scores, axis=-1, keepdims=True)
    e = jnp.exp(scores - top)
    probs = e / jnp.sum(e, axis=-1, keepdims=True)
    probs_b = probs.astype(BF)
    attn = jnp.einsum("hqt,td->qhd", probs_b, v, preferred_element_type=F32)
    attn = attn.reshape(span, -1).astype(BF)
    middle = hidden + rows_sum(mm(attn, out_all))
    scale_two = lax.rsqrt(jnp.mean(middle * middle, axis=-1, keepdims=True) + EPS)
    n2 = rows_gather((middle * scale_two * gain_two).astype(BF))
    gate = mm(n2, gate_all)
    up = mm(n2, up_all)
    sig = jax.nn.sigmoid(gate)
    inner = (gate * sig * up).astype(BF)
    block_out = (keep * (middle + rows_sum(mm(inner, down_all)))).astype(BF)
    grad_down = mm(inner, g_all, 0, 0)
    g_inner = mm(g_all, down_all, 1, 1)
    g_gate = (g_inner * up * sig * (1.0 + gate * (1.0 - sig))).astype(BF)
    g_up = (g_inner * gate * sig).astype(BF)
    g_n2 = rows_sum(mm(g_gate, gate_all, 1, 1) + mm(g_up, up_all, 1, 1))
    grad_gate = mm(n2, g_gate, 0, 0)
    grad_up = mm(n2, g_up, 0, 0)
    d_mid, grad_gain_two = norm_back(g_n2, middle, scale_two, gain_two)
    g_mid = g_out + d_mid
    gm_all = rows_gather(g_mid.astype(BF))
    grad_out = mm(attn, gm_all, 0, 0)
    g_attn = mm(gm_all, out_all, 1, 1).astype(BF).reshape(span, -1, hd)
    dp = jnp.einsum("qhd,td->hqt", g_attn, v, preferred_element_type=F32)
    delta = jnp.sum(probs * dp, axis=-1, keepdims=True)
    ds = (probs * (dp - delta)).astype(BF)
    g_q = jnp.einsum("hqt,td->qhd", ds, k, preferred_element_type=F32) * scale
    g_k = jnp.einsum("hqt,qhd->td", ds, q, preferred_element_type=F32) * scale
    g_v = jnp.einsum("hqt,qhd->td", probs_b, g_attn, preferred_element_type=F32)
    g_kv = lax.psum_scatter(
        jnp.concatenate([g_k, g_v], axis=1), "context", scatter_dimension=0, tiled=True
    )
    g_q = rotate(g_q, cos_t, -sin_t).astype(BF).reshape(span, -1)
    g_k = rotate(g_kv[:, None, :hd], cos_t, -sin_t).astype(BF)[:, 0]
    g_qkv = jnp.concatenate([g_q, g_k, g_kv[:, hd:].astype(BF)], axis=1)
    g_n1 = rows_sum(mm(g_qkv, qkv_all, 1, 1))
    grad_qkv = mm(n1, g_qkv, 0, 0)
    d_hid, grad_gain_one = norm_back(g_n1, hidden, scale_one, gain_one)
    gains = jnp.stack([grad_gain_one, grad_gain_two])
    return (block_out, g_mid + d_hid, gains, grad_qkv, grad_out, grad_gate, grad_up, grad_down)


def body(
    hidden_in,
    segment_ids,
    pad_mask,
    attn_gain,
    w_query,
    w_key,
    w_value,
    w_out,
    mlp_gain,
    w_gate,
    w_up,
    w_down,
    cotangent,
):
    block_out, grad_hidden, gains, grad_qkv, grad_out, grad_gate, grad_up, grad_down = one_sequence(
        hidden_in[0],
        segment_ids[0],
        pad_mask[0],
        attn_gain,
        w_query,
        w_key,
        w_value,
        w_out,
        mlp_gain,
        w_gate,
        w_up,
        w_down,
        cotangent[0],
    )
    grad_down = scatter_g(grad_down, 1)
    grad_gate = scatter_g(grad_gate)
    grad_up = scatter_g(grad_up)
    grad_out = scatter_g(grad_out, 1)
    grad_qkv = scatter_g(grad_qkv)
    gains = lax.psum(gains, "tensor")
    gains = lax.psum_scatter(gains, FC, scatter_dimension=1, tiled=True)
    qw, hd = (w_query.shape[1], w_key.shape[1])
    return (
        block_out[None],
        grad_hidden[None],
        gains[0],
        grad_qkv[:, :qw],
        grad_qkv[:, qw : qw + hd],
        grad_qkv[:, qw + hd :],
        grad_out,
        gains[1],
        grad_gate,
        grad_up,
        grad_down,
    )


def solution(mesh):
    fc = ("fsdp", "context")
    rows = P("fsdp", ("context", "tensor"), None)
    tail = (
        P(fc),
        P(fc, "tensor"),
        P(fc, "tensor"),
        P(fc, "tensor"),
        P("tensor", fc),
        P(fc),
        P(fc, "tensor"),
        P(fc, "tensor"),
        P("tensor", fc),
    )
    in_specs = (rows, P("fsdp", None), P("fsdp", None)) + tail + (rows,)
    out_specs = (rows, rows) + tail
    return jax.shard_map(body, mesh=mesh, in_specs=in_specs, out_specs=out_specs, check_vma=False)
```

profile of v0, /device:TPU:0, one launch (start us, length us, event | category | flops | bytes accessed | tf_op | source)
XLA Modules:
  0.0 838.9 jit_solution(12737155059699517862)
XLA Ops:
  9.0 10.3 %all-gather = bf16[8,1,256]{2,1,0:T(2,128)(2,1)S(1)} all-gather(bf16[1,1,256]{2,1,0:T(2,128)(2,1)S(1)} %reshape.348), channel_id=1, replica_groups=mesh['fsdp'=2,'context'=4,'tensor'=4] {'fsdp','context'}, dimensions={0}, use_global_device_ids=true | all-gather | bytes 4608 | tf_op jit(solution)/shard_map/all_gather | solution.py:49
  29.8 19.8 %all-gather.12.cloned.1.call-done = bf16[256,2048]{1,0:T(8,128)(2,1)} async-done(((bf16[64,2048]{1,0:T(8,128)(2,1)}), bf16[256,2048]{1,0:T(8,128)(2,1)}) %all-gather.12.cloned.1.call-update) | async-done | bytes 1048592 | tf_op jit(solution)/shard_map/all_gather | solution.py:38
  49.6 32.1 %all-gather.14.cloned.1.call-done = bf16[2048,640]{1,0:T(8,128)(2,1)} async-done(((bf16[256,640]{1,0:T(8,128)(2,1)}), bf16[2048,640]{1,0:T(8,128)(2,1)}) %all-gather.14.cloned.1.call-update) | async-done | bytes 2621456 | tf_op jit(solution)/shard_map/all_gather | solution.py:49
  85.8 5.8 all_gather.39
  100.8 11.0 %all-gather.16.cloned.1.call-done = bf16[512,2048]{1,0:T(8,128)(2,1)} async-done(((bf16[512,256]{1,0:T(8,128)(2,1)}), bf16[512,2048]{1,0:T(8,128)(2,1)}) %all-gather.16.cloned.1.call-update) | async-done | bytes 2097168 | tf_op jit(solution)/shard_map/all_gather | solution.py:49
  115.2 8.8 %all-gather.1 = bf16[8,1,256]{2,1,0:T(2,128)(2,1)S(1)} all-gather(bf16[1,1,256]{2,1,0:T(2,128)(2,1)S(1)} %reshape.350), channel_id=1, replica_groups=mesh['fsdp'=2,'context'=4,'tensor'=4] {'fsdp','context'}, dimensions={0}, use_global_device_ids=true | all-gather | bytes 4608 | tf_op jit(solution)/shard_map/all_gather | solution.py:49
  124.0 18.4 %reduce-scatter.14.cloned.1.call-done = bf16[64,2048]{1,0:T(8,128)(2,1)} async-done(((bf16[256,2048]{1,0:T(8,128)(2,1)}), bf16[64,2048]{1,0:T(8,128)(2,1)}) %reduce-scatter.14.cloned.1.call-update) | async-done | bytes 262160 | tf_op jit(solution)/shard_map/reduce_scatter | solution.py:42
  149.3 22.8 %all-gather.18.cloned.1.call-done = bf16[256,2048]{1,0:T(8,128)(2,1)} async-done(((bf16[64,2048]{1,0:T(8,128)(2,1)}), bf16[256,2048]{1,0:T(8,128)(2,1)}) %all-gather.18.cloned.1.call-update) | async-done | bytes 1048592 | tf_op jit(solution)/shard_map/all_gather | solution.py:38
  172.1 44.7 %all-gather.22.cloned.1.call-done = bf16[2048,1408]{1,0:T(8,128)(2,1)} async-done(((bf16[256,1408]{1,0:T(8,128)(2,1)}), bf16[2048,1408]{1,0:T(8,128)(2,1)}) %all-gather.22.cloned.1.call-update) | async-done | bytes 5767184 | tf_op jit(solution)/shard_map/all_gather | solution.py:49
  216.8 5.9 fusion.86
  222.7 39.5 %all-gather.20.cloned.1.call-done = bf16[2048,1408]{1,0:T(8,128)(2,1)} async-done(((bf16[256,1408]{1,0:T(8,128)(2,1)}), bf16[2048,1408]{1,0:T(8,128)(2,1)}) %all-gather.20.cloned.1.call-update) | async-done | bytes 5767184 | tf_op jit(solution)/shard_map/all_gather | solution.py:49
  262.2 5.5 fusion.85
  267.8 24.7 %all-gather.26.cloned.1.call-done = bf16[256,2048]{1,0:T(8,128)(2,1)} async-done(((bf16[64,2048]{1,0:T(8,128)(2,1)}), bf16[256,2048]{1,0:T(8,128)(2,1)}) %all-gather.26.cloned.1.call-update) | async-done | bytes 1048592 | tf_op jit(solution)/shard_map/all_gather | solution.py:38
  292.4 45.9 %all-gather.24.cloned.1.call-done = bf16[1408,2048]{1,0:T(8,128)(2,1)} async-done(((bf16[1408,256]{1,0:T(8,128)(2,1)}), bf16[1408,2048]{1,0:T(8,128)(2,1)}) %all-gather.24.cloned.1.call-update) | async-done | bytes 5767184 | tf_op jit(solution)/shard_map/all_gather | solution.py:49
  338.3 6.2 multiply_convert_fusion
  346.5 5.5 fusion.8
  352.0 27.2 %reduce-scatter.18.cloned.1.call-done = bf16[64,2048]{1,0:T(8,128)(2,1)} async-done(((bf16[256,2048]{1,0:T(8,128)(2,1)}), bf16[64,2048]{1,0:T(8,128)(2,1)}) %reduce-scatter.18.cloned.1.call-update) | async-done | bytes 262160 | tf_op jit(solution)/shard_map/reduce_scatter | solution.py:42
  382.8 26.5 %all-gather.28.cloned.1.call-done = bf16[256,2048]{1,0:T(8,128)(2,1)} async-done(((bf16[64,2048]{1,0:T(8,128)(2,1)}), bf16[256,2048]{1,0:T(8,128)(2,1)}) %all-gather.28.cloned.1.call-update) | async-done | bytes 1048592 | tf_op jit(solution)/shard_map/all_gather | solution.py:38
  414.4 4.9 fusion.17
  419.4 4.8 fusion.1
  432.9 18.1 %reduce-scatter.20.cloned.1.call-done = f32[256,128]{0,1:T(8,128)} async-done(((f32[1024,128]{0,1:T(8,128)}), f32[256,128]{0,1:T(8,128)}) %reduce-scatter.20.cloned.1.call-update) | async-done | bytes 131088 | tf_op jit(solution)/shard_map/reduce_scatter | solution.py:156
  460.1 5.4 convolution_convert_fusion.7
  465.6 18.3 %reduce-scatter.22.cloned.1.call-done = bf16[64,2048]{1,0:T(8,128)(2,1)} async-done(((bf16[256,2048]{1,0:T(8,128)(2,1)}), bf16[64,2048]{1,0:T(8,128)(2,1)}) %reduce-scatter.22.cloned.1.call-update) | async-done | bytes 262160 | tf_op jit(solution)/shard_map/reduce_scatter | solution.py:42
  489.3 5.6 convolution_convert_fusion
  505.8 21.1 %reduce-scatter.26.cloned.1.call-done = bf16[512,256]{1,0:T(8,128)(2,1)} async-done(((bf16[512,2048]{1,0:T(8,128)(2,1)}), bf16[512,256]{1,0:T(8,128)(2,1)}) %reduce-scatter.26.cloned.1.call-update) | async-done | bytes 262160 | tf_op jit(solution)/shard_map/reduce_scatter | solution.py:53
  528.8 28.2 %reduce-scatter.16.cloned.1.call-done = bf16[64,2048]{1,0:T(8,128)(2,1)} async-done(((bf16[256,2048]{1,0:T(8,128)(2,1)}), bf16[64,2048]{1,0:T(8,128)(2,1)}) %reduce-scatter.16.cloned.1.call-update) | async-done | bytes 262160 | tf_op jit(solution)/shard_map/reduce_scatter | solution.py:42
  559.4 35.9 %reduce-scatter.34.cloned.1.call-done = f32[256,2]{1,0:T(8,128)} async-done(((f32[2048,2]{1,0:T(8,128)}), f32[256,2]{1,0:T(8,128)}) %reduce-scatter.34.cloned.1.call-update) | async-done | bytes 2064
  596.3 11.7 %psum.8 = f32[2,256]{1,0:T(2,128)S(1)} all-reduce(f32[2,256]{1,0:T(2,128)S(1)} %copy.113), channel_id=1, replica_groups=mesh['fsdp'=2,'context'=4,'tensor'=4] {'tensor'}, use_global_device_ids=true, to_apply=%region_15.16 | all-reduce | flops 512 | bytes 4096 | tf_op jit(solution)/shard_map/psum | solution.py:204
  608.6 33.6 %reduce-scatter.24.cloned.1.call-done = bf16[256,640]{1,0:T(8,128)(2,1)} async-done(((bf16[2048,640]{1,0:T(8,128)(2,1)}), bf16[256,640]{1,0:T(8,128)(2,1)}) %reduce-scatter.24.cloned.1.call-update) | async-done | bytes 327696 | tf_op jit(solution)/shard_map/reduce_scatter | solution.py:53
  646.4 58.1 %reduce-scatter.32.cloned.1.call-done = bf16[1408,256]{1,0:T(8,128)(2,1)} async-done(((bf16[1408,2048]{1,0:T(8,128)(2,1)}), bf16[1408,256]{1,0:T(8,128)(2,1)}) %reduce-scatter.32.cloned.1.call-update) | async-done | bytes 720912 | tf_op jit(solution)/shard_map/reduce_scatter | solution.py:53
  706.8 60.6 %reduce-scatter.30.cloned.1.call-done = bf16[256,1408]{1,0:T(8,128)(2,1)} async-done(((bf16[2048,1408]{1,0:T(8,128)(2,1)}), bf16[256,1408]{1,0:T(8,128)(2,1)}) %reduce-scatter.30.cloned.1.call-update) | async-done | bytes 720912 | tf_op jit(solution)/shard_map/reduce_scatter | solution.py:53
  769.7 60.1 %reduce-scatter.28.cloned.1.call-done = bf16[256,1408]{1,0:T(8,128)(2,1)} async-done(((bf16[2048,1408]{1,0:T(8,128)(2,1)}), bf16[256,1408]{1,0:T(8,128)(2,1)}) %reduce-scatter.28.cloned.1.call-update) | async-done | bytes 720912 | tf_op jit(solution)/shard_map/reduce_scatter | solution.py:53
  (149 shorter events, 96.8 us)
Async XLA Ops:
  7.2 42.4 %all-gather.12.cloned.1.call-start = ((), (), s32[]{:S(2)}) async-start(), calls=%async_computation.11 | async-start | bytes 1310720 | tf_op jit(solution)/shard_map/all_gather | solution.py:38
  21.2 60.5 %all-gather.14.cloned.1.call-start = ((), (), s32[]{:S(2)}) async-start(), calls=%async_computation.12 | async-start | bytes 2949120 | tf_op jit(solution)/shard_map/all_gather | solution.py:49
  24.8 87.0 %all-gather.16.cloned.1.call-start = ((), (), s32[]{:S(2)}) async-start(), calls=%async_computation.13 | async-start | bytes 2359296 | tf_op jit(solution)/shard_map/all_gather | solution.py:49
  25.5 116.9 %reduce-scatter.14.cloned.1.call-start = ((), (), s32[]{:S(2)}) async-start(), calls=%async_computation.14 | async-start | bytes 1310720 | tf_op jit(solution)/shard_map/reduce_scatter | solution.py:42
  100.8 14.4 %copy-start.15 = (bf16[256]{0:T(256)(128)(2,1)S(1)}, bf16[256]{0:T(256)(128)(2,1)}, u32[]{:S(2)}) copy-start(bf16[256]{0:T(256)(128)(2,1)} %param.21) | copy-start | bytes 1540
  100.8 41.6 %copy-start.1 = (bf16[1,64,2048]{2,1,0:T(8,128)(2,1)S(1)}, bf16[1,64,2048]{2,1,0:T(8,128)(2,1)}, u32[]{:S(2)}) copy-start(bf16[1,64,2048]{2,1,0:T(8,128)(2,1)} %param.13) | copy-start | bytes 786436
  100.8 46.7 %copy-start.5 = (bf16[1,64,2048]{2,1,0:T(8,128)(2,1)S(1)}, bf16[1,64,2048]{2,1,0:T(8,128)(2,1)}, u32[]{:S(2)}) copy-start(bf16[1,64,2048]{2,1,0:T(8,128)(2,1)} %param.25) | copy-start | bytes 786436
  115.1 57.0 %all-gather.18.cloned.1.call-start = ((), (), s32[]{:S(2)}) async-start(), calls=%async_computation.15 | async-start | bytes 1310720 | tf_op jit(solution)/shard_map/all_gather | solution.py:38
  145.4 71.5 %all-gather.22.cloned.1.call-start = ((), (), s32[]{:S(2)}) async-start(), calls=%async_computation.17 | async-start | bytes 6488064 | tf_op jit(solution)/shard_map/all_gather | solution.py:49
  145.9 116.3 %all-gather.20.cloned.1.call-start = ((), (), s32[]{:S(2)}) async-start(), calls=%async_computation.16 | async-start | bytes 6488064 | tf_op jit(solution)/shard_map/all_gather | solution.py:49
  146.7 145.7 %all-gather.26.cloned.1.call-start = ((), (), s32[]{:S(2)}) async-start(), calls=%async_computation.20 | async-start | bytes 1310720 | tf_op jit(solution)/shard_map/all_gather | solution.py:38
  148.3 190.0 %all-gather.24.cloned.1.call-start = ((), (), s32[]{:S(2)}) async-start(), calls=%async_computation.18 | async-start | bytes 6488064 | tf_op jit(solution)/shard_map/all_gather | solution.py:49
  149.1 230.2 %reduce-scatter.18.cloned.1.call-start = ((), (), s32[]{:S(2)}) async-start(), calls=%async_computation.21 | async-start | bytes 1310720 | tf_op jit(solution)/shard_map/reduce_scatter | solution.py:42
  172.1 90.1 %copy-start.2 = (bf16[256,2048]{1,0:T(8,128)(2,1)S(1)}, bf16[256,2048]{1,0:T(8,128)(2,1)}, u32[]{:S(2)}) copy-start(bf16[256,2048]{1,0:T(8,128)(2,1)} %all-gather.18.cloned.1.call-done) | copy-start | bytes 3145732
  338.3 6.3 copy-start.14
  344.6 115.5 %copy-start.7 = (bf16[256,1408]{1,0:T(8,128)(2,1)}, bf16[256,1408]{1,0:T(8,128)(2,1)S(1)}, u32[]{:S(2)}) copy-start(bf16[256,1408]{1,0:T(8,128)(2,1)S(1)} %get-tuple-element.61) | copy-start | bytes 2162692
  346.4 32.8 %copy-start.3 = (bf16[64,2048]{1,0:T(8,128)(2,1)S(1)}, bf16[64,2048]{1,0:T(8,128)(2,1)}, u32[]{:S(2)}) copy-start(bf16[64,2048]{1,0:T(8,128)(2,1)} %reduce-scatter.14.cloned.1.call-done) | copy-start | bytes 786436
  352.0 57.3 %all-gather.28.cloned.1.call-start = ((), (), s32[]{:S(2)}) async-start(), calls=%async_computation.22 | async-start | bytes 1310720 | tf_op jit(solution)/shard_map/all_gather | solution.py:38
  382.5 68.5 %reduce-scatter.20.cloned.1.call-start = ((), (), s32[]{:S(2)}) async-start(), calls=%async_computation.23 | async-start | bytes 655360 | tf_op jit(solution)/shard_map/reduce_scatter | solution.py:156
  414.4 4.9 copy-start.13
  414.4 9.8 %slice-start = ((s8[8388608]{0:T(1024)(128)(4,1)}), s8[4194304]{0:T(1024)(128)(4,1)S(1)}, s32[]{:S(2)}) async-start(s8[8388608]{0:T(1024)(128)(4,1)} %bitcast.139), calls=%async_computation.31 | async-start | bytes 8388608
  429.7 54.3 %reduce-scatter.22.cloned.1.call-start = ((), (), s32[]{:S(2)}) async-start(), calls=%async_computation.24 | async-start | bytes 1310720 | tf_op jit(solution)/shard_map/reduce_scatter | solution.py:42
  456.7 70.3 %reduce-scatter.26.cloned.1.call-start = ((), (), s32[]{:S(2)}) async-start(), calls=%async_computation.26 | async-start | bytes 2359296 | tf_op jit(solution)/shard_map/reduce_scatter | solution.py:53
  460.1 96.9 %reduce-scatter.16.cloned.1.call-start = ((), (), s32[]{:S(2)}) async-start(), calls=%async_computation.19 | async-start | bytes 1310720 | tf_op jit(solution)/shard_map/reduce_scatter | solution.py:42
  465.5 21.1 %copy-start.4 = (bf16[256,2048]{1,0:T(8,128)(2,1)S(1)}, bf16[256,2048]{1,0:T(8,128)(2,1)}, u32[]{:S(2)}) copy-start(bf16[256,2048]{1,0:T(8,128)(2,1)} %all-gather.12.cloned.1.call-done) | copy-start | bytes 3145732
  465.6 129.7 %reduce-scatter.34.cloned.1.call-start = ((), (), s32[]{:S(2)}) async-start(), calls=%async_computation.30 | async-start | bytes 1179648
  486.6 155.5 %reduce-scatter.24.cloned.1.call-start = ((), (), s32[]{:S(2)}) async-start(), calls=%async_computation.25 | async-start | bytes 2949120 | tf_op jit(solution)/shard_map/reduce_scatter | solution.py:53
  489.2 215.3 %reduce-scatter.32.cloned.1.call-start = ((), (), s32[]{:S(2)}) async-start(), calls=%async_computation.29 | async-start | bytes 6488064 | tf_op jit(solution)/shard_map/reduce_scatter | solution.py:53
  494.9 272.5 %reduce-scatter.30.cloned.1.call-start = ((), (), s32[]{:S(2)}) async-start(), calls=%async_computation.28 | async-start | bytes 6488064 | tf_op jit(solution)/shard_map/reduce_scatter | solution.py:53
  500.4 329.4 %reduce-scatter.28.cloned.1.call-start = ((), (), s32[]{:S(2)}) async-start(), calls=%async_computation.27 | async-start | bytes 6488064 | tf_op jit(solution)/shard_map/reduce_scatter | solution.py:53
  505.8 51.2 %copy-start.6 = (bf16[64,2048]{1,0:T(8,128)(2,1)S(1)}, bf16[64,2048]{1,0:T(8,128)(2,1)}, u32[]{:S(2)}) copy-start(bf16[64,2048]{1,0:T(8,128)(2,1)} %reduce-scatter.18.cloned.1.call-done) | copy-start | bytes 786436
  505.8 51.2 %copy-start.8 = (bf16[64,2048]{1,0:T(8,128)(2,1)S(1)}, bf16[64,2048]{1,0:T(8,128)(2,1)}, u32[]{:S(2)}) copy-start(bf16[64,2048]{1,0:T(8,128)(2,1)} %reduce-scatter.22.cloned.1.call-done) | copy-start | bytes 786436
  (6 other events, 12.8 us)
Sparse Core Ops, SparseCore 0:
  21.3 28.2 all-gather.11
  52.0 29.6 all-gather.13
  83.6 28.1 all-gather.15
  115.2 27.1 reduce-scatter.13
  145.5 26.5 all-gather.17
  174.0 42.7 all-gather.21
  218.9 43.3 all-gather.19
  264.5 27.9 all-gather.25
  294.5 43.8 all-gather.23
  352.1 27.1 reduce-scatter.17
  382.6 26.5 all-gather.27
  429.8 21.1 reduce-scatter.19
  456.8 27.1 reduce-scatter.21
  487.1 39.8 reduce-scatter.25
  529.8 27.1 reduce-scatter.15
  560.6 34.6 reduce-scatter.33
  598.5 43.6 reduce-scatter.23
  645.5 59.0 reduce-scatter.31
  708.4 59.0 reduce-scatter.29
  770.7 59.0 reduce-scatter.27
where the time goes:
time: 840 us; the launch traced here: 839 us
  waiting for transfers between devices  650 us (77%)
  matrix products  87.3 us (10%)
  blocking collectives  36.7 us (4%)
  other arithmetic  30.9 us (4%)
  local copies, waits for them, and re-layouts  18.2 us (2%)
  between operations  14.8 us (2%)
    reduce_scatter x5, waiting for transfers between devices, scatter_g(): lax.psum_scatter(g.astype(BF), FC, scatter_dimension=axis, tiled=True)  234 us
    all_gather x5, waiting for transfers between devices, gather_w(): return lax.all_gather(w, FC, axis=axis, tiled=True)  173 us
    all_gather x4, waiting for transfers between devices, rows_gather(): return lax.all_gather(x, 'tensor', axis=0, tiled=True)  93.7 us
    reduce_scatter x4, waiting for transfers between devices, rows_sum(): lax.psum_scatter(x.astype(BF), 'tensor', scatter_dimension=0, tiled=True)  92.2 us
    dot_general x15, matrix products, mm(): lax.dot_general(a, b, (((ca,), (cb,)), ((), ())), preferred_element_type=...  64 us
    unnamed x21, waiting for transfers between devices  38.8 us
    all_gather x2, blocking collectives, gather_w(): return lax.all_gather(w, FC, axis=axis, tiled=True)  19.2 us
    reduce_scatter x1, waiting for transfers between devices, one_sequence(): lax.psum_scatter(jnp.concatenate([g_k, g_v], axis=1), 'context', scatter_...  18.1 us
  transfers between devices with their start and end apart: 20, of which 20 were waited for; matrix products, arithmetic and copies ran while one was open for 10% of the time, Pallas kernels for 0%

commit v1 on v0

--- a/solution.py
+++ b/solution.py
@@ -8,6 +8,15 @@
 NEG = -1e30
 BF = jnp.bfloat16
 F32 = jnp.float32
+
+
+def save_bars(target, out_dim):
+    target = jnp.moveaxis(target, 0, out_dim)
+    met_up = target.shape
+    known = target.reshape(
+        *met_up[:out_dim], met_up[out_dim] * met_up[out_dim + 1], *met_up[out_dim + 2 :]
+    )
+    return known
 
 
 def rope_tables(positions, head_size):
@@ -35,7 +44,27 @@
 
 
 def rows_gather(x):
-    return lax.all_gather(x, "tensor", axis=0, tiled=True)
+
+    def expand_table(tile_in, axis_key, dim_k):
+        sides = lax.axis_size(axis_key)
+        xs_all = tuple(((kk, (kk + 1) % sides) for kk in range(sides)))
+        leaves = tuple(((t, i) for i, t in xs_all))
+        far_arr, answer = ([], [])
+        for ii in range(sides - 1):
+            if ii % 2 == 0:
+                far_arr.append(lax.ppermute(far_arr[-1] if far_arr else tile_in, axis_key, xs_all))
+            else:
+                outcome_arr = lax.ppermute(answer[-1] if answer else tile_in, axis_key, leaves)
+                answer.append(outcome_arr)
+        part_next = jnp.stack([*far_arr[::-1], tile_in, *answer], axis=0)
+        low = lax.axis_index(axis_key)
+        plain = len(far_arr)
+        d_next = low - plain
+        part_next = part_next[(jnp.arange(sides) - d_next) % sides]
+        z2 = save_bars(part_next, dim_k)
+        return z2
+
+    return expand_table(x, "tensor", 0)
 
 
 def rows_sum(x):

time: 840 us -> 742 us (0.88)
  waiting for transfers between devices: 650 us -> 521 us
  starting transfers between devices: 1.48 us -> 19.3 us
    all_gather x4 -> x0, waiting for transfers between devices: 93.7 us -> none  [rows_gather(): return lax.all_gather(x, 'tensor', axis=0, tiled=True)]
    all_gather x5, waiting for transfers between devices: 173 us -> 87.7 us  [gather_w(): return lax.all_gather(w, FC, axis=axis, tiled=True)]
    ppermute x0 -> x12, waiting for transfers between devices: none -> 53.8 us  [the longest x8 46.2 us: expand_table(): lax.ppermute(far_arr[-1] if far_arr else tile_in, axis_key, xs_all)]
    reduce_scatter x4, waiting for transfers between devices: 92.2 us -> 69.2 us  [rows_sum(): lax.psum_scatter(x.astype(BF), 'tensor', scatter_dimension=0, tiled=True)]
    reduce_scatter x5, waiting for transfers between devices: 234 us -> 254 us  [scatter_g(): lax.psum_scatter(g.astype(BF), FC, scatter_dimension=axis, tiled=True)]
    ppermute x0 -> x12, starting transfers between devices: none -> 18.4 us  [the longest x4 14.5 us: expand_table(): lax.ppermute(answer[-1] if answer else tile_in, axis_key, leaves)]
    unnamed x21 -> x17, waiting for transfers between devices: 38.8 us -> 39.7 us
  transfers between devices with their start and end apart: 20 -> 28, of which waited for: 20 -> 25; matrix products, arithmetic and copies ran while one was open for 10% -> 12% of each run, Pallas kernels for 0% -> 0%
where the time goes in v1:
time: 742 us; the launch traced here: 741 us
  waiting for transfers between devices  521 us (70%)
  matrix products  87.7 us (12%)
  blocking collectives  37.4 us (5%)
  other arithmetic  35 us (5%)
  local copies, waits for them, and re-layouts  26 us (4%)
  starting transfers between devices  19.3 us (3%)
  between operations  14.7 us (2%)
    reduce_scatter x5, waiting for transfers between devices, scatter_g(): lax.psum_scatter(g.astype(BF), FC, scatter_dimension=axis, tiled=True)  254 us
    all_gather x5, waiting for transfers between devices, gather_w(): return lax.all_gather(w, FC, axis=axis, tiled=True)  87.7 us
    reduce_scatter x4, waiting for transfers between devices, rows_sum(): lax.psum_scatter(x.astype(BF), 'tensor', scatter_dimension=0, tiled=True)  69.2 us
    dot_general x15, matrix products, mm(): lax.dot_general(a, b, (((ca,), (cb,)), ((), ())), preferred_element_type=...  64.4 us
    ppermute x8, waiting for transfers between devices, expand_table(): lax.ppermute(far_arr[-1] if far_arr else tile_in, axis_key, xs_all)  46.2 us
    unnamed x17, waiting for transfers between devices  39.7 us
    all_gather x2, blocking collectives, gather_w(): return lax.all_gather(w, FC, axis=axis, tiled=True)  19.2 us
    reduce_scatter x1, waiting for transfers between devices, one_sequence(): lax.psum_scatter(jnp.concatenate([g_k, g_v], axis=1), 'context', scatter_...  16.7 us
  transfers between devices with their start and end apart: 28, of which 25 were waited for; matrix products, arithmetic and copies ran while one was open for 12% of the time, Pallas kernels for 0%

profile of v1, /device:TPU:0, one launch (start us, length us, event | category | flops | bytes accessed | tf_op | source)
XLA Modules:
  0.0 740.7 jit_solution(16984137720217957004)
XLA Ops:
  11.5 10.3 %all-gather = bf16[8,1,256]{2,1,0:T(2,128)(2,1)S(1)} all-gather(bf16[1,1,256]{2,1,0:T(2,128)(2,1)S(1)} %reshape.465), channel_id=1, replica_groups=mesh['fsdp'=2,'context'=4,'tensor'=4] {'fsdp','context'}, dimensions={0}, use_global_device_ids=true | all-gather | bytes 4608 | tf_op jit(solution)/shard_map/all_gather | solution.py:78
  32.1 8.2 %collective-permute-done = bf16[64,2048]{1,0:T(8,128)(2,1)S(1)} collective-permute-done((bf16[64,2048]{1,0:T(8,128)(2,1)S(1)}, bf16[64,2048]{1,0:T(8,128)(2,1)S(1)}, u32[]{:S(2)}, u32[]{:S(2)}) %collective-permute-start) | collective-permute-done | bytes 262176 | tf_op jit(solution)/shard_map/ppermute | solution.py:55
  43.6 6.2 collective-permute-done.1
  54.4 6.5 all_gather.26
  61.0 4.8 fusion.92
  81.4 8.8 %all-gather.1 = bf16[8,1,256]{2,1,0:T(2,128)(2,1)S(1)} all-gather(bf16[1,1,256]{2,1,0:T(2,128)(2,1)S(1)} %reshape.467), channel_id=1, replica_groups=mesh['fsdp'=2,'context'=4,'tensor'=4] {'fsdp','context'}, dimensions={0}, use_global_device_ids=true | all-gather | bytes 4608 | tf_op jit(solution)/shard_map/all_gather | solution.py:78
  90.2 17.7 %reduce-scatter.14.cloned.1.call-done = bf16[64,2048]{1,0:T(8,128)(2,1)} async-done(((bf16[256,2048]{1,0:T(8,128)(2,1)}), bf16[64,2048]{1,0:T(8,128)(2,1)}) %reduce-scatter.14.cloned.1.call-update) | async-done | bytes 262160 | tf_op jit(solution)/shard_map/reduce_scatter | solution.py:71
  126.0 6.5 collective-permute-done.7
  135.8 7.2 collective-permute-done.4
  151.4 5.5 fusion.95
  156.9 39.7 %all-gather.12.cloned.1.call-done = bf16[2048,1408]{1,0:T(8,128)(2,1)} async-done(((bf16[256,1408]{1,0:T(8,128)(2,1)}), bf16[2048,1408]{1,0:T(8,128)(2,1)}) %all-gather.12.cloned.1.call-update) | async-done | bytes 5767184 | tf_op jit(solution)/shard_map/all_gather | solution.py:78
  196.6 5.5 fusion.94
  202.2 40.7 %all-gather.16.cloned.1.call-done = bf16[1408,2048]{1,0:T(8,128)(2,1)} async-done(((bf16[1408,256]{1,0:T(8,128)(2,1)}), bf16[1408,2048]{1,0:T(8,128)(2,1)}) %all-gather.16.cloned.1.call-update) | async-done | bytes 5767184 | tf_op jit(solution)/shard_map/all_gather | solution.py:78
  242.9 7.1 multiply_convert_fusion
  251.9 5.5 fusion.8
  257.5 27.2 %reduce-scatter.18.cloned.1.call-done = bf16[64,2048]{1,0:T(8,128)(2,1)} async-done(((bf16[256,2048]{1,0:T(8,128)(2,1)}), bf16[64,2048]{1,0:T(8,128)(2,1)}) %reduce-scatter.18.cloned.1.call-update) | async-done | bytes 262160 | tf_op jit(solution)/shard_map/reduce_scatter | solution.py:71
  292.2 7.2 collective-permute-done.9
  301.9 7.4 collective-permute-done.10
  317.9 4.9 fusion.17
  322.8 4.8 fusion.1
  336.4 16.7 %reduce-scatter.20.cloned.1.call-done = f32[256,128]{0,1:T(8,128)} async-done(((f32[1024,128]{0,1:T(8,128)}), f32[256,128]{0,1:T(8,128)}) %reduce-scatter.20.cloned.1.call-update) | async-done | bytes 131088 | tf_op jit(solution)/shard_map/reduce_scatter | solution.py:185
  358.9 5.7 convolution_convert_fusion.7
  368.1 18.1 %reduce-scatter.22.cloned.1.call-done = bf16[64,2048]{1,0:T(8,128)(2,1)} async-done(((bf16[256,2048]{1,0:T(8,128)(2,1)}), bf16[64,2048]{1,0:T(8,128)(2,1)}) %reduce-scatter.22.cloned.1.call-update) | async-done | bytes 262160 | tf_op jit(solution)/shard_map/reduce_scatter | solution.py:71
  391.5 5.6 convolution_convert_fusion
  408.0 6.1 reduce-scatter.16.cloned.1.call-done
  416.5 41.2 %reduce-scatter.26.cloned.1.call-done = bf16[512,256]{1,0:T(8,128)(2,1)} async-done(((bf16[512,2048]{1,0:T(8,128)(2,1)}), bf16[512,256]{1,0:T(8,128)(2,1)}) %reduce-scatter.26.cloned.1.call-update) | async-done | bytes 262160 | tf_op jit(solution)/shard_map/reduce_scatter | solution.py:82
  459.5 37.9 %reduce-scatter.34.cloned.1.call-done = f32[256,2]{1,0:T(8,128)} async-done(((f32[2048,2]{1,0:T(8,128)}), f32[256,2]{1,0:T(8,128)}) %reduce-scatter.34.cloned.1.call-update) | async-done | bytes 2064
  498.3 11.7 %psum.8 = f32[2,256]{1,0:T(2,128)S(1)} all-reduce(f32[2,256]{1,0:T(2,128)S(1)} %copy.113), channel_id=1, replica_groups=mesh['fsdp'=2,'context'=4,'tensor'=4] {'tensor'}, use_global_device_ids=true, to_apply=%region_15.16 | all-reduce | flops 512 | bytes 4096 | tf_op jit(solution)/shard_map/psum | solution.py:233
  510.6 33.7 %reduce-scatter.24.cloned.1.call-done = bf16[256,640]{1,0:T(8,128)(2,1)} async-done(((bf16[2048,640]{1,0:T(8,128)(2,1)}), bf16[256,640]{1,0:T(8,128)(2,1)}) %reduce-scatter.24.cloned.1.call-update) | async-done | bytes 327696 | tf_op jit(solution)/shard_map/reduce_scatter | solution.py:82
  548.6 58.2 %reduce-scatter.32.cloned.1.call-done = bf16[1408,256]{1,0:T(8,128)(2,1)} async-done(((bf16[1408,2048]{1,0:T(8,128)(2,1)}), bf16[1408,256]{1,0:T(8,128)(2,1)}) %reduce-scatter.32.cloned.1.call-update) | async-done | bytes 720912 | tf_op jit(solution)/shard_map/reduce_scatter | solution.py:82
  609.0 60.4 %reduce-scatter.30.cloned.1.call-done = bf16[256,1408]{1,0:T(8,128)(2,1)} async-done(((bf16[2048,1408]{1,0:T(8,128)(2,1)}), bf16[256,1408]{1,0:T(8,128)(2,1)}) %reduce-scatter.30.cloned.1.call-update) | async-done | bytes 720912 | tf_op jit(solution)/shard_map/reduce_scatter | solution.py:82
  671.8 60.1 %reduce-scatter.28.cloned.1.call-done = bf16[256,1408]{1,0:T(8,128)(2,1)} async-done(((bf16[2048,1408]{1,0:T(8,128)(2,1)}), bf16[256,1408]{1,0:T(8,128)(2,1)}) %reduce-scatter.28.cloned.1.call-update) | async-done | bytes 720912 | tf_op jit(solution)/shard_map/reduce_scatter | solution.py:82
  (217 shorter events, 138.5 us)
Async XLA Ops:
  7.2 43.4 %all-gather.8.cloned.1.call-start = ((), (), s32[]{:S(2)}) async-start(), calls=%async_computation.11 | async-start | bytes 2949120 | tf_op jit(solution)/shard_map/all_gather | solution.py:78
  10.8 63.1 %all-gather.10.cloned.1.call-start = ((), (), s32[]{:S(2)}) async-start(), calls=%async_computation.12 | async-start | bytes 2359296 | tf_op jit(solution)/shard_map/all_gather | solution.py:78
  24.0 19.5 %collective-permute-start.2 = (bf16[64,2048]{1,0:T(8,128)(2,1)S(1)}, bf16[64,2048]{1,0:T(8,128)(2,1)S(1)}, u32[]{:S(2)}, u32[]{:S(2)}) collective-permute-start(bf16[64,2048]{1,0:T(8,128)(2,1)S(1)} %fusion.43), channel_id=1, source_target_pairs={{1,0},{2,1},{3,2},{0,3},{5,4},{6,5},{7,6},{4,7},{9,8},{10,9},{11,1... | collective-permute-start | bytes 786440 | tf_op jit(solution)/shard_map/ppermute | solution.py:57
  27.7 12.6 %collective-permute-start = (bf16[64,2048]{1,0:T(8,128)(2,1)S(1)}, bf16[64,2048]{1,0:T(8,128)(2,1)S(1)}, u32[]{:S(2)}, u32[]{:S(2)}) collective-permute-start(bf16[64,2048]{1,0:T(8,128)(2,1)S(1)} %fusion.43), channel_id=1, source_target_pairs={{0,1},{1,2},{2,3},{3,0},{4,5},{5,6},{6,7},{7,4},{8,9},{9,10},{10,1... | collective-permute-start | bytes 786440 | tf_op jit(solution)/shard_map/ppermute | solution.py:55
  27.7 80.2 %reduce-scatter.14.cloned.1.call-start = ((), (), s32[]{:S(2)}) async-start(), calls=%async_computation.13 | async-start | bytes 1310720 | tf_op jit(solution)/shard_map/reduce_scatter | solution.py:71
  40.3 9.5 %collective-permute-start.1 = (bf16[64,2048]{1,0:T(8,128)(2,1)S(1)}, bf16[64,2048]{1,0:T(8,128)(2,1)S(1)}, u32[]{:S(2)}, u32[]{:S(2)}) collective-permute-start(bf16[64,2048]{1,0:T(8,128)(2,1)S(1)} %collective-permute-done), channel_id=1, source_target_pairs={{0,1},{1,2},{2,3},{3,0},{4,5},{5,6},{6,7},{7,4},{8,9},{9,10},{10,1... | collective-permute-start | bytes 786440 | tf_op jit(solution)/shard_map/ppermute | solution.py:55
  70.8 39.4 %copy-start.6 = (bf16[64,8,256]{2,0,1:T(8,128)(2,1)}, bf16[64,8,256]{2,0,1:T(8,128)(2,1)S(1)}, u32[]{:S(2)}) copy-start(bf16[64,8,256]{2,0,1:T(8,128)(2,1)S(1)} %fusion.14) | copy-start | bytes 786436
  70.8 37.1 %copy-start.1 = (bf16[1,64,2048]{2,1,0:T(8,128)(2,1)S(1)}, bf16[1,64,2048]{2,1,0:T(8,128)(2,1)}, u32[]{:S(2)}) copy-start(bf16[1,64,2048]{2,1,0:T(8,128)(2,1)} %param.13) | copy-start | bytes 786436
  77.2 74.2 %all-gather.14.cloned.1.call-start = ((), (), s32[]{:S(2)}) async-start(), calls=%async_computation.15 | async-start | bytes 6488064 | tf_op jit(solution)/shard_map/all_gather | solution.py:78
  77.7 118.9 %all-gather.12.cloned.1.call-start = ((), (), s32[]{:S(2)}) async-start(), calls=%async_computation.14 | async-start | bytes 6488064 | tf_op jit(solution)/shard_map/all_gather | solution.py:78
  78.3 164.6 %all-gather.16.cloned.1.call-start = ((), (), s32[]{:S(2)}) async-start(), calls=%async_computation.16 | async-start | bytes 6488064 | tf_op jit(solution)/shard_map/all_gather | solution.py:78
  78.9 205.8 %reduce-scatter.18.cloned.1.call-start = ((), (), s32[]{:S(2)}) async-start(), calls=%async_computation.18 | async-start | bytes 1310720 | tf_op jit(solution)/shard_map/reduce_scatter | solution.py:71
  79.7 52.8 %copy-start.24 = (f32[64]{0:T(128)}, f32[64]{0:T(128)S(1)}, u32[]{:S(2)}) copy-start(f32[64]{0:T(128)S(1)} %convert_bitcast_fusion.2) | copy-start | bytes 772
  79.8 34.2 %collective-permute-start.6 = (bf16[64,2048]{1,0:T(8,128)(2,1)S(1)}, bf16[64,2048]{1,0:T(8,128)(2,1)S(1)}, u32[]{:S(2)}, u32[]{:S(2)}) collective-permute-start(bf16[64,2048]{1,0:T(8,128)(2,1)S(1)} %fusion.50), channel_id=1, source_target_pairs={{0,1},{1,2},{2,3},{3,0},{4,5},{5,6},{6,7},{7,4},{8,9},{9,10},{10,1... | collective-permute-start | bytes 786440 | tf_op jit(solution)/shard_map/ppermute | solution.py:55
  110.2 11.2 %collective-permute-start.3 = (bf16[64,2048]{1,0:T(8,128)(2,1)S(1)}, bf16[64,2048]{1,0:T(8,128)(2,1)}, u32[]{:S(2)}, u32[]{:S(2)}) collective-permute-start(bf16[64,2048]{1,0:T(8,128)(2,1)S(1)} %multiply_convert_fusion.4), channel_id=1, source_target_pairs={{0,1},{1,2},{2,3},{3,0},{4,5},{5,6},{6,7},{7,4},{8,9},{9,10},{10,1... | collective-permute-start | bytes 786440 | tf_op jit(solution)/shard_map/ppermute | solution.py:55
  110.8 15.2 %collective-permute-start.8 = (bf16[64,2048]{1,0:T(8,128)(2,1)S(1)}, bf16[64,2048]{1,0:T(8,128)(2,1)S(1)}, u32[]{:S(2)}, u32[]{:S(2)}) collective-permute-start(bf16[64,2048]{1,0:T(8,128)(2,1)S(1)} %fusion.50), channel_id=1, source_target_pairs={{1,0},{2,1},{3,2},{0,3},{5,4},{6,5},{7,6},{4,7},{9,8},{10,9},{11,1... | collective-permute-start | bytes 786440 | tf_op jit(solution)/shard_map/ppermute | solution.py:57
  114.1 18.5 %collective-permute-start.7 = (bf16[64,2048]{1,0:T(8,128)(2,1)S(1)}, bf16[64,2048]{1,0:T(8,128)(2,1)S(1)}, u32[]{:S(2)}, u32[]{:S(2)}) collective-permute-start(bf16[64,2048]{1,0:T(8,128)(2,1)S(1)} %collective-permute-done.6), channel_id=1, source_target_pairs={{0,1},{1,2},{2,3},{3,0},{4,5},{5,6},{6,7},{7,4},{8,9},{9,10},{10,1... | collective-permute-start | bytes 786440 | tf_op jit(solution)/shard_map/ppermute | solution.py:55
  114.1 21.7 %collective-permute-start.5 = (bf16[64,2048]{1,0:T(8,128)(2,1)S(1)}, bf16[64,2048]{1,0:T(8,128)(2,1)}, u32[]{:S(2)}, u32[]{:S(2)}) collective-permute-start(bf16[64,2048]{1,0:T(8,128)(2,1)S(1)} %multiply_convert_fusion.4), channel_id=1, source_target_pairs={{1,0},{2,1},{3,2},{0,3},{5,4},{6,5},{7,6},{4,7},{9,8},{10,9},{11,1... | collective-permute-start | bytes 786440 | tf_op jit(solution)/shard_map/ppermute | solution.py:57
  121.3 21.7 %collective-permute-start.4 = (bf16[64,2048]{1,0:T(8,128)(2,1)}, bf16[64,2048]{1,0:T(8,128)(2,1)}, u32[]{:S(2)}, u32[]{:S(2)}) collective-permute-start(bf16[64,2048]{1,0:T(8,128)(2,1)} %collective-permute-done.3), channel_id=1, source_target_pairs={{0,1},{1,2},{2,3},{3,0},{4,5},{5,6},{6,7},{7,4},{8,9},{9,10},{10,1... | collective-permute-start | bytes 786440 | tf_op jit(solution)/shard_map/ppermute | solution.py:55
  251.9 35.2 %copy-start.25 = (f32[64]{0:T(128)S(1)}, f32[64]{0:T(128)}, u32[]{:S(2)}) copy-start(f32[64]{0:T(128)} %copy-done.24) | copy-start | bytes 772
  257.4 95.7 %reduce-scatter.20.cloned.1.call-start = ((), (), s32[]{:S(2)}) async-start(), calls=%async_computation.19 | async-start | bytes 655360 | tf_op jit(solution)/shard_map/reduce_scatter | solution.py:185
  288.3 11.1 %collective-permute-start.9 = (bf16[64,2048]{1,0:T(8,128)(2,1)S(1)}, bf16[64,2048]{1,0:T(8,128)(2,1)S(1)}, u32[]{:S(2)}, u32[]{:S(2)}) collective-permute-start(bf16[64,2048]{1,0:T(8,128)(2,1)S(1)} %fusion.89), channel_id=1, source_target_pairs={{0,1},{1,2},{2,3},{3,0},{4,5},{5,6},{6,7},{7,4},{8,9},{9,10},{10,1... | collective-permute-start | bytes 786440 | tf_op jit(solution)/shard_map/ppermute | solution.py:55
  288.4 13.6 %collective-permute-start.11 = (bf16[64,2048]{1,0:T(8,128)(2,1)S(1)}, bf16[64,2048]{1,0:T(8,128)(2,1)S(1)}, u32[]{:S(2)}, u32[]{:S(2)}) collective-permute-start(bf16[64,2048]{1,0:T(8,128)(2,1)S(1)} %fusion.89), channel_id=1, source_target_pairs={{1,0},{2,1},{3,2},{0,3},{5,4},{6,5},{7,6},{4,7},{9,8},{10,9},{11,1... | collective-permute-start | bytes 786440 | tf_op jit(solution)/shard_map/ppermute | solution.py:57
  299.4 10.0 %collective-permute-start.10 = (bf16[64,2048]{1,0:T(8,128)(2,1)S(1)}, bf16[64,2048]{1,0:T(8,128)(2,1)S(1)}, u32[]{:S(2)}, u32[]{:S(2)}) collective-permute-start(bf16[64,2048]{1,0:T(8,128)(2,1)S(1)} %collective-permute-done.9), channel_id=1, source_target_pairs={{0,1},{1,2},{2,3},{3,0},{4,5},{5,6},{6,7},{7,4},{8,9},{9,10},{10,1... | collective-permute-start | bytes 786440 | tf_op jit(solution)/shard_map/ppermute | solution.py:55
  333.2 52.9 %reduce-scatter.22.cloned.1.call-start = ((), (), s32[]{:S(2)}) async-start(), calls=%async_computation.20 | async-start | bytes 1310720 | tf_op jit(solution)/shard_map/reduce_scatter | solution.py:71
  358.9 55.3 %reduce-scatter.16.cloned.1.call-start = ((), (), s32[]{:S(2)}) async-start(), calls=%async_computation.17 | async-start | bytes 1310720 | tf_op jit(solution)/shard_map/reduce_scatter | solution.py:71
  364.6 93.0 %reduce-scatter.26.cloned.1.call-start = ((), (), s32[]{:S(2)}) async-start(), calls=%async_computation.22 | async-start | bytes 2359296 | tf_op jit(solution)/shard_map/reduce_scatter | solution.py:82
  368.0 129.3 %reduce-scatter.34.cloned.1.call-start = ((), (), s32[]{:S(2)}) async-start(), calls=%async_computation.26 | async-start | bytes 1179648
  388.8 155.5 %reduce-scatter.24.cloned.1.call-start = ((), (), s32[]{:S(2)}) async-start(), calls=%async_computation.21 | async-start | bytes 2949120 | tf_op jit(solution)/shard_map/reduce_scatter | solution.py:82
  391.4 215.3 %reduce-scatter.32.cloned.1.call-start = ((), (), s32[]{:S(2)}) async-start(), calls=%async_computation.25 | async-start | bytes 6488064 | tf_op jit(solution)/shard_map/reduce_scatter | solution.py:82
  397.1 272.3 %reduce-scatter.30.cloned.1.call-start = ((), (), s32[]{:S(2)}) async-start(), calls=%async_computation.24 | async-start | bytes 6488064 | tf_op jit(solution)/shard_map/reduce_scatter | solution.py:82
  402.6 329.3 %reduce-scatter.28.cloned.1.call-start = ((), (), s32[]{:S(2)}) async-start(), calls=%async_computation.23 | async-start | bytes 6488064 | tf_op jit(solution)/shard_map/reduce_scatter | solution.py:82
  (36 other events, 409.5 us)
Sparse Core Ops, SparseCore 0:
  10.9 32.8 all-gather.7
  45.6 28.1 all-gather.9
  77.3 30.6 reduce-scatter.13
  109.8 41.5 all-gather.13
  153.3 43.3 all-gather.11
  198.5 44.3 all-gather.15
  257.6 27.1 reduce-scatter.17
  333.3 19.8 reduce-scatter.19
  359.0 27.1 reduce-scatter.21
  388.3 25.7 reduce-scatter.15
  417.8 39.8 reduce-scatter.25
  461.3 35.9 reduce-scatter.33
  500.6 43.6 reduce-scatter.23
  547.6 59.0 reduce-scatter.31
  610.4 59.0 reduce-scatter.29
  672.8 59.0 reduce-scatter.27
